TPU v7x, 32 devices: a whole 2x2x4 slice. The times are simulated.
32 devices in a mesh: tm: 4 (over y, x), vox: 8 (over z, core).
Axes of the slice: x: 2, y: 2, z: 4, core: 2. Of those that a mesh axis runs over, the one named last changes fastest.
Arguments:
- u_train: bfloat16 [3072, 4096], P('tm'), may hold values from -0.109375 to 0.109375
- y_train: bfloat16 [3072, 3072], P('tm', 'vox'), may hold values from -6 to 6
- sing: float32 [4096], replicated, may hold values from 0.5 to 8
- lambdas: float32 [20], replicated, may hold values from 0.1 to 100
- lam_index: int32 [24], P('vox'), may hold values from 0 to 19
- live: int32 [24], P('vox'), may hold values from 0 to 1, as said below
- v_basis: bfloat16 [4096, 4096], P('tm', 'vox'), may hold values from -0.09375 to 0.09375
- x_test: bfloat16 [1024, 4096], P(None, 'tm'), may hold values from -0.09375 to 0.09375
Outputs:
- weights: bfloat16 [4096, 3072], P('tm', 'vox')
- predictions: bfloat16 [1024, 3072], P('tm', 'vox')
Inputs may be any that keep to these rules, and one draw needn't show every extreme that they name: Of the 3 voxel blocks that one device along vox holds, at most 2 are live, and some device holds exactly 2.
All inputs are finite; a program needn't handle non-finite values.
Results may differ from a plain program's by a relative error of at most 0.0058.
Values may be sent and summed in bfloat16 or wider, within the bound.
A program may use at most 128 MiB of HBM per device.

v0:
```python
import jax
import jax.numpy as jnp
from jax import lax
from jax.sharding import PartitionSpec as P

BLK = 128


def body(u_train, y_train, sing, lambdas, lam_index, live, v_basis, x_test):
    time_rows = y_train.shape[0]
    column_count = y_train.shape[1]
    block_count = lam_index.shape[0]
    penalty_count = lambdas.shape[0]
    capacity = block_count - block_count // 3
    selector = (lam_index[:, None] == jnp.arange(penalty_count, dtype=jnp.int32)[None, :]).astype(
        jnp.float32
    )
    selector = selector * live[:, None].astype(jnp.float32)
    ranking = jnp.argsort((1 - live) * block_count + jnp.arange(block_count, dtype=jnp.int32))
    picked = ranking[:capacity]
    responses = jnp.take(y_train.reshape(time_rows, block_count, BLK), picked, axis=1)
    responses = responses.reshape(time_rows, capacity * BLK)
    used_selector = jnp.take(selector, picked, axis=0)
    used_columns = responses.shape[1]
    used_blocks = used_selector.shape[0]
    partial_value = lax.dot_general(
        u_train, responses, (((0,), (0,)), ((), ())), preferred_element_type=jnp.float32
    )
    products = lax.psum(partial_value, "tm")
    filters = sing[None, :] / (sing[None, :] * sing[None, :] + lambdas[:, None])
    row_count = products.shape[0]
    blocks = (
        products.reshape(row_count, used_blocks, BLK)
        * jnp.dot(used_selector, filters, precision=lax.Precision.HIGHEST).T[:, :, None]
    )
    filtered = blocks.reshape(row_count, used_columns).astype(jnp.bfloat16)
    weight_sum = jnp.dot(
        lax.all_gather(v_basis, "vox", axis=1, tiled=True),
        filtered,
        preferred_element_type=jnp.float32,
    )
    weight_cols = weight_sum.astype(jnp.bfloat16)
    partial_test = jnp.dot(x_test, weight_cols, preferred_element_type=jnp.float32)
    predicted = lax.psum_scatter(partial_test, "tm", scatter_dimension=0, tiled=True).astype(
        jnp.bfloat16
    )

    def expand(values):
        row_count = values.shape[0]
        placed = jnp.zeros((row_count, block_count, BLK), values.dtype)
        placed = placed.at[:, picked, :].set(values.reshape(row_count, capacity, BLK))
        return placed.reshape(row_count, column_count)

    return (expand(weight_cols), expand(predicted))


def solution(mesh):
    placed = (
        P("tm", None),
        P("tm", "vox"),
        P(),
        P(),
        P("vox"),
        P("vox"),
        P("tm", "vox"),
        P(None, "tm"),
    )
    return jax.shard_map(
        body,
        mesh=mesh,
        in_specs=placed,
        out_specs=(P("tm", "vox"), P("tm", "vox")),
        check_vma=False,
    )
```

profile of v0, /device:TPU:0, one launch (start us, length us, event | category | flops | bytes accessed | tf_op | source)
XLA Modules:
  0.0 177.4 jit_solution(16627243049810682810)
XLA Ops:
  8.0 0.0 copy-start
  8.0 0.0 all-reduce.2.cloned.1.call-start
  8.1 0.8 fusion.10
  8.9 0.7 sort.17
  9.6 1.3 copy.20
  10.9 0.3 copy.21
  11.3 1.3 gather_fusion
  12.6 1.2 copy.22
  13.8 0.1 broadcast_bitcast_fusion
  13.8 0.1 bitcast_select_fusion
  14.0 6.6 %convolution_bitcast_fusion = f32[4096,256]{0,1:T(8,128)} fusion(bf16[768,256]{0,1:T(8,128)(2,1)S(1)} %bitcast_select_fusion, bf16[768,4096]{1,0:T(8,128)(2,1)} %param.8), kind=kOutput, calls=%fused_computation.4 | convolution fusion | flops 1610612736 | bytes 10878976 | tf_op jit(solution)/shard_map/dot_general | solution.py:26
  20.6 0.0 copy-start.2
  20.6 0.0 copy-start.1
  20.6 0.0 copy-start.3
  20.6 0.0 all-reduce.2.cloned.1.call-update
  20.6 0.0 all-gather.2.cloned.1.call-start
  20.7 0.5 all-gather.2.cloned.1.call-update
  21.2 0.0 reduce-scatter.2.cloned.1.call-start
  21.3 0.0 copy-done.2
  21.3 0.1 fusion.5
  21.3 0.6 gather_fusion.1
  21.9 0.0 copy-done.1
  21.9 0.0 copy-done.3
  21.9 0.5 fusion.1
  22.4 104.7 %all-reduce.2.cloned.1.call-done = f32[4096,256]{0,1:T(8,128)} async-done(((f32[4096,256]{0,1:T(8,128)}), f32[4096,256]{0,1:T(8,128)}) %all-reduce.2.cloned.1.call-update) | async-done | bytes 4194320 | tf_op jit(solution)/shard_map/psum | solution.py:29
  127.1 3.9 %fusion = bf16[4096,256]{0,1:T(8,128)(2,1)} fusion(f32[4096,256]{0,1:T(8,128)} %all-reduce.2.cloned.1.call-done, f32[4096,2]{0,1:T(2,128)S(1)} %fusion.1), kind=kLoop, calls=%fused_computation.6 | loop fusion | flops 2097152 | bytes 6324224 | tf_op jit(solution)/shard_map/convert_element_type | solution.py:36
  131.0 0.0 all-gather.2.cloned.1.call-done
  131.0 6.4 %convolution_convert_fusion = bf16[256,1024]{1,0:T(8,128)(2,1)S(1)} fusion(bf16[4096,256]{0,1:T(8,128)(2,1)} %fusion, bf16[1024,4096]{1,0:T(8,128)(2,1)} %all-gather.2.cloned.1.call-done), kind=kOutput, calls=%fused_computation.8 | convolution fusion | flops 2147745792 | bytes 11010048 | tf_op jit(solution)/shard_map/dot_general | solution.py:37
  137.4 0.0 copy-done
  137.4 1.7 convolution_bitcast_fusion.1
  139.1 0.0 reduce-scatter.2.cloned.1.call-update
  139.2 0.3 copy.23
  139.4 0.1 broadcast_in_dim.42
  139.6 0.7 scatter_fusion
  140.3 1.2 copy.24
  141.5 2.3 %copy.27 = bf16[1024,384]{1,0:T(8,128)(2,1)} copy(bf16[1024,384]{0,1:T(8,128)(2,1)} %bitcast.28) | data formatting | bytes 1572864
  143.8 23.4 %reduce-scatter.2.cloned.1.call-done = f32[256,256]{0,1:T(8,128)} async-done(((f32[1024,256]{0,1:T(8,128)}), f32[256,256]{0,1:T(8,128)}) %reduce-scatter.2.cloned.1.call-update) | async-done | bytes 262160 | tf_op jit(solution)/shard_map/reduce_scatter | solution.py:44
  167.3 1.0 convert_element_type.21
  168.2 0.1 copy.25
  168.4 0.6 scatter_fusion.1
  169.0 0.1 copy.26
  169.2 0.8 copy.28
  (5 shorter events, 0.0 us)
Async XLA Ops:
  8.0 129.4 %copy-start = (bf16[1024,1024]{1,0:T(8,128)(2,1)S(1)}, bf16[1024,1024]{1,0:T(8,128)(2,1)}, u32[]{:S(2)}) copy-start(bf16[1024,1024]{1,0:T(8,128)(2,1)} %param.15) | copy-start | bytes 6291460
  8.0 119.1 %all-reduce.2.cloned.1.call-start = ((), (), s32[]{:S(2)}) async-start(), calls=%async_computation.1 | async-start | bytes 8388608 | tf_op jit(solution)/shard_map/psum | solution.py:29
  20.6 0.7 copy-start.2
  20.6 1.3 copy-start.1
  20.6 1.3 copy-start.3
  20.6 110.4 %all-gather.2.cloned.1.call-start = ((), (), s32[]{:S(2)}) async-start(), calls=%async_computation.2 | async-start | bytes 9437184 | tf_op jit(solution)/shard_map/all_gather | solution.py:38
  21.2 146.1 %reduce-scatter.2.cloned.1.call-start = ((), (), s32[]{:S(2)}) async-start(), calls=%async_computation.3 | async-start | bytes 1310720 | tf_op jit(solution)/shard_map/reduce_scatter | solution.py:44
Sparse Core Ops, SparseCore 0:
  20.7 106.3 all-reduce.1
  139.3 27.9 reduce-scatter.1
Sparse Core Ops, SparseCore 1:
  22.7 84.6 all-gather.1
where the time goes:
time: 178 us; the launch traced here: 177 us
  waiting for transfers between devices  129 us (72%)
  between operations  15.6 us (9%)
  matrix products  15.2 us (9%)
  local copies, waits for them, and re-layouts  11.1 us (6%)
  other arithmetic  6.63 us (4%)
    psum x1, waiting for transfers between devices, body(): products = lax.psum(partial_value, 'tm')  105 us
    reduce_scatter x1, waiting for transfers between devices, body(): lax.psum_scatter(partial_test, 'tm', scatter_dimension=0, tiled=True)  23.4 us
    dot_general x1, matrix products, body(): lax.dot_general(u_train, responses, (((0,), (0,)), ((), ())), preferred_e...  6.63 us
    dot_general x1, matrix products, body(): jnp.dot(lax.all_gather(v_basis, 'vox', axis=1, tiled=True), filtered, pre...  6.38 us
    unnamed x11, local copies, waits for them, and re-layouts  4.43 us
    convert_element_type x1, other arithmetic, body(): filtered = blocks.reshape(row_count, used_columns).astype(jnp.bfloat16)  3.9 us
  transfers between devices with their start and end apart: 3, of which 2 were waited for; matrix products, arithmetic and copies ran while one was open for 5% of the time, Pallas kernels for 0%

commit v1 on v0

v1 whole, which is shorter than its diff:
```python
import functools

import jax
import jax.numpy as jnp
from jax import lax
from jax.experimental import pallas as pl
from jax.experimental.pallas import tpu as pltpu
from jax.sharding import PartitionSpec as P

BLK = 128
CHUNKS = 4
TILE = 256
MESH = pl.DeviceIdType.MESH


def kernel(
    n_t,
    n_v,
    cap,
    live_ref,
    index_ref,
    lambda_ref,
    sing_ref,
    y_ref,
    u_ref,
    v_ref,
    x_ref,
    w_ref,
    pred_ref,
    u_buf,
    x_buf,
    v_all,
    part_out,
    part_in,
    part_own,
    filt,
    acc,
    pred_acc,
    pred_out,
    pred_in,
    u_sem,
    x_sem,
    own_sem,
    right_sem,
    left_sem,
    line_sem,
    pair_send,
    pair_recv,
    rs_send,
    rs_recv,
    ag_send,
    ag_recv,
    q_send,
    q_recv,
):
    t = lax.axis_index("tm")
    v = lax.axis_index("vox")
    n_z = n_v // 2
    z, core = v // 2, v % 2
    mate = z * 2 + 1 - core
    rows_v, depth = v_ref.shape
    blocks = live_ref.shape[0]
    share = part_own.shape[1]
    test_rows = pred_out.shape[1]
    rc = rows_v // CHUNKS

    def u_copy(owner):
        cols = pl.ds(pl.multiple_of(owner * share, share), share)
        return pltpu.make_async_copy(u_ref.at[:, cols], u_buf.at[:, cols], u_sem.at[owner])

    def own_copy(ch):
        rows = pl.ds(ch * rc, rc)
        return pltpu.make_async_copy(v_ref.at[rows], v_all.at[v, rows], own_sem.at[ch])

    def line_copy(src, ch, step, first=False):
        rows = pl.ds(ch * rc, rc)
        slot = src * 2 + core
        return pltpu.make_async_remote_copy(
            src_ref=v_ref.at[rows] if first else v_all.at[slot, rows],
            dst_ref=v_all.at[slot, rows],
            send_sem=(right_sem if step > 0 else left_sem).at[src, ch],
            recv_sem=line_sem.at[src, ch],
            device_id={"vox": v + 2 * step},
            device_id_type=MESH,
        )

    def pair_copy(src, ch, first=False):
        rows = pl.ds(ch * rc, rc)
        slot = src * 2 + core
        return pltpu.make_async_remote_copy(
            src_ref=v_ref.at[rows] if first else v_all.at[slot, rows],
            dst_ref=v_all.at[slot, rows],
            send_sem=pair_send.at[src, ch],
            recv_sem=pair_recv.at[src, ch],
            device_id={"vox": mate},
            device_id_type=MESH,
        )

    def pair_arrival(src, ch):
        rows = pl.ds(ch * rc, rc)
        slot = src * 2 + 1 - core
        return pltpu.make_async_remote_copy(
            src_ref=v_all.at[slot, rows],
            dst_ref=v_all.at[slot, rows],
            send_sem=pair_send.at[src, ch],
            recv_sem=pair_recv.at[src, ch],
            device_id={"vox": mate},
            device_id_type=MESH,
        )

    def peer(d):
        return lax.rem(t + d, n_t)

    def part_copy(to, owner):
        return pltpu.make_async_remote_copy(
            src_ref=part_out.at[to],
            dst_ref=part_in.at[owner],
            send_sem=rs_send.at[to],
            recv_sem=rs_recv.at[owner],
            device_id={"tm": to},
            device_id_type=MESH,
        )

    def filt_copy(to, owner):
        return pltpu.make_async_remote_copy(
            src_ref=filt.at[owner],
            dst_ref=filt.at[owner],
            send_sem=ag_send.at[to],
            recv_sem=ag_recv.at[owner],
            device_id={"tm": to},
            device_id_type=MESH,
        )

    def pred_copy(to, owner):
        return pltpu.make_async_remote_copy(
            src_ref=pred_out.at[to],
            dst_ref=pred_in.at[owner],
            send_sem=q_send.at[to],
            recv_sem=q_recv.at[owner],
            device_id={"tm": to},
            device_id_type=MESH,
        )

    for d in range(n_t):
        u_copy(peer((d + 1) % n_t)).start()

    barrier = pltpu.get_barrier_semaphore()
    for d in range(1, n_t):
        pl.semaphore_signal(barrier, inc=1, device_id={"tm": peer(d)}, device_id_type=MESH)
    pl.semaphore_signal(barrier, inc=1, device_id={"vox": mate}, device_id_type=MESH)

    @pl.when(z > 0)
    def _():
        pl.semaphore_signal(barrier, inc=1, device_id={"vox": v - 2}, device_id_type=MESH)

    @pl.when(z < n_z - 1)
    def _():
        pl.semaphore_signal(barrier, inc=1, device_id={"vox": v + 2}, device_id_type=MESH)

    neighbours = jnp.where(z > 0, 1, 0) + jnp.where(z < n_z - 1, 1, 0)
    pl.semaphore_wait(barrier, n_t + neighbours)

    for ch in range(CHUNKS):

        @pl.when(z > 0)
        def _():
            line_copy(z, ch, -1, True).start()

        @pl.when(z < n_z - 1)
        def _():
            line_copy(z, ch, 1, True).start()

    live = [live_ref[i] for i in range(blocks)]
    before = [sum(live[:i], jnp.int32(0)) for i in range(blocks)]
    pick = [
        [jnp.where(before[i] == j, live[i], 0).astype(jnp.float32) for i in range(blocks)]
        for j in range(cap)
    ]
    lam = [lambda_ref[index_ref[i]] for i in range(blocks)]
    slot_lam = [sum(pick[j][i] * lam[i] for i in range(blocks)) for j in range(cap)]
    slot_live = [sum(pick[j][i] for i in range(blocks)) for j in range(cap)]

    y_cols = [y_ref[:, i * BLK : (i + 1) * BLK].astype(jnp.float32) for i in range(blocks)]
    y_t = jnp.concatenate(
        [sum(pick[j][i] * y_cols[i] for i in range(blocks)).T for j in range(cap)], axis=0
    ).astype(jnp.bfloat16)

    for d in range(1, n_t + 1):
        to = peer(d % n_t)
        u_copy(to).wait()

        def tile(i, _, to=to, d=d):
            off = pl.multiple_of(i * TILE, TILE)
            cols = pl.ds(pl.multiple_of(to * share + i * TILE, TILE), TILE)
            value = jnp.dot(y_t, u_buf[:, cols], preferred_element_type=jnp.float32)
            if d < n_t:
                part_out[to, :, pl.ds(off, TILE)] = value.astype(jnp.bfloat16)
            else:
                part_own[:, pl.ds(off, TILE)] = value
            return 0

        lax.fori_loop(0, share // TILE, tile, 0)
        if d < n_t:
            part_copy(to, t).start()

    for ch in range(CHUNKS):
        pair_copy(z, ch, True).start()
        own_copy(ch).start()
    x_copy = pltpu.make_async_copy(x_ref, x_buf, x_sem)
    x_copy.start()

    def relay(s, ch):
        low, high = z - 1 - s, z + 1 + s

        @pl.when(low >= 0)
        def _():
            line_copy(low, ch, -1).wait_recv()

            @pl.when(z < n_z - 1)
            def _():
                line_copy(low, ch, 1).start()

            pair_copy(low, ch).start()

        @pl.when(high < n_z)
        def _():
            line_copy(high, ch, 1).wait_recv()

            @pl.when(z > 0)
            def _():
                line_copy(high, ch, -1).start()

            pair_copy(high, ch).start()

    for ch in range(CHUNKS // 2):
        relay(0, ch)

    for d in range(1, n_t):
        part_copy(peer(d), peer(d)).wait_recv()
    for i in range(share // TILE):
        cols = slice(i * TILE, (i + 1) * TILE)
        sing = sing_ref[:, pl.ds(pl.multiple_of(t * share + i * TILE, TILE), TILE)]
        for j in range(cap):
            rows = slice(j * BLK, (j + 1) * BLK)
            total = part_own[rows, cols]
            for d in range(1, n_t):
                total = total + part_in[peer(d), rows, cols].astype(jnp.float32)
            factor = sing / (sing * sing + slot_lam[j]) * slot_live[j]
            filt[t, rows, cols] = (total * factor).astype(jnp.bfloat16)
    for d in range(1, n_t):
        filt_copy(peer(d), t).start()

    for ch in range(CHUNKS // 2, CHUNKS):
        relay(0, ch)

    def relay_step(s, _):
        for ch in range(CHUNKS):
            relay(s, ch)
        return 0

    lax.fori_loop(1, n_z - 2, relay_step, 0)

    for d in range(1, n_t):
        filt_copy(peer(d), peer(d)).wait_recv()

    def term(src, ch):
        pair_arrival(src, ch).wait_recv()
        rows = pl.ds(ch * rc, rc)
        value = None
        for c in range(2):
            slot = src * 2 + c
            start = slot * depth
            owner = start // share
            offset = pl.multiple_of(start - owner * share, depth)
            part = lax.dot_general(
                v_all[slot, rows, :],
                filt[owner, :, pl.ds(offset, depth)],
                (((1,), (1,)), ((), ())),
                preferred_element_type=jnp.float32,
            )
            value = part if value is None else value + part
        return value

    for ch in range(CHUNKS):
        own_copy(ch).wait()
        acc[pl.ds(ch * rc, rc), :] = term(z, ch)

    def add_step(s, _):
        low, high = z - 1 - s, z + 1 + s
        for ch in range(CHUNKS):
            rows = pl.ds(ch * rc, rc)

            @pl.when(low >= 0)
            def _():
                acc[rows, :] += term(low, ch)

            @pl.when(high < n_z)
            def _():
                acc[rows, :] += term(high, ch)

        return 0

    lax.fori_loop(0, n_z - 2, add_step, 0)
    x_copy.wait()

    def expand(values):
        return [
            sum(pick[j][i] * values[:, j * BLK : (j + 1) * BLK] for j in range(cap))
            for i in range(blocks)
        ]

    def finish(ch):
        rows = slice(ch * rc, (ch + 1) * rc)

        @pl.when(z == 0)
        def _():
            acc[rows, :] += term(n_z - 1, ch)

        @pl.when(z == n_z - 1)
        def _():
            acc[rows, :] += term(0, ch)

        weights = acc[rows, :].astype(jnp.bfloat16)
        for i, block in enumerate(expand(weights.astype(jnp.float32))):
            w_ref[rows, i * BLK : (i + 1) * BLK] = block.astype(jnp.bfloat16)
        value = jnp.dot(x_buf[:, rows], weights, preferred_element_type=jnp.float32)
        if ch == 0:
            pred_acc[...] = value
        else:
            pred_acc[...] += value

    for ch in range(CHUNKS):
        relay(n_z - 2, ch)
        if ch > 0:
            finish(ch - 1)
    finish(CHUNKS - 1)

    for d in range(1, n_t):
        to = peer(d)
        mine = pl.ds(pl.multiple_of(to * test_rows, test_rows), test_rows)
        pred_out[to] = pred_acc[mine, :].astype(jnp.bfloat16)
        pred_copy(to, t).start()
    for d in range(1, n_t):
        pred_copy(peer(d), peer(d)).wait_recv()
    total = pred_acc[pl.ds(pl.multiple_of(t * test_rows, test_rows), test_rows), :]
    for d in range(1, n_t):
        total = total + pred_in[peer(d)].astype(jnp.float32)
    for i, block in enumerate(expand(total)):
        pred_ref[:, i * BLK : (i + 1) * BLK] = block.astype(jnp.bfloat16)

    for d in range(1, n_t):
        part_copy(peer(d), t).wait_send()
        filt_copy(peer(d), t).wait_send()
        pred_copy(peer(d), t).wait_send()

    def drain(src, _):
        for ch in range(CHUNKS):
            pair_copy(src, ch).wait_send()

            @pl.when((src <= z) & (z < n_z - 1))
            def _():
                line_copy(src, ch, 1).wait_send()

            @pl.when((src >= z) & (z > 0))
            def _():
                line_copy(src, ch, -1).wait_send()

        return 0

    lax.fori_loop(0, n_z, drain, 0)


def body(n_t, n_v, u_train, y_train, sing, lambdas, lam_index, live, v_basis, x_test):
    time_rows, features = u_train.shape
    columns = y_train.shape[1]
    blocks = lam_index.shape[0]
    cap = blocks - blocks // 3
    used = cap * BLK
    rows_v, depth = v_basis.shape
    tests = x_test.shape[0]
    share = features // n_t
    n_z = n_v // 2
    low, full = jnp.bfloat16, jnp.float32
    smem = pl.BlockSpec(memory_space=pltpu.SMEM)
    vmem = pl.BlockSpec(memory_space=pltpu.VMEM)
    anywhere = pl.BlockSpec(memory_space=pl.ANY)
    dma = pltpu.SemaphoreType.DMA
    return pl.pallas_call(
        functools.partial(kernel, n_t, n_v, cap),
        out_shape=(
            jax.ShapeDtypeStruct((rows_v, columns), low),
            jax.ShapeDtypeStruct((tests // n_t, columns), low),
        ),
        in_specs=[smem, smem, smem, vmem, vmem, anywhere, anywhere, anywhere],
        out_specs=(vmem, vmem),
        scratch_shapes=[
            pltpu.VMEM((time_rows, features), low),
            pltpu.VMEM((tests, rows_v), low),
            pltpu.VMEM((n_v, rows_v, depth), low),
            pltpu.VMEM((n_t, used, share), low),
            pltpu.VMEM((n_t, used, share), low),
            pltpu.VMEM((used, share), full),
            pltpu.VMEM((n_t, used, share), low),
            pltpu.VMEM((rows_v, used), full),
            pltpu.VMEM((tests, used), full),
            pltpu.VMEM((n_t, tests // n_t, used), low),
            pltpu.VMEM((n_t, tests // n_t, used), low),
            dma((n_t,)),
            dma,
            dma((CHUNKS,)),
            dma((n_z, CHUNKS)),
            dma((n_z, CHUNKS)),
            dma((n_z, CHUNKS)),
            dma((n_z, CHUNKS)),
            dma((n_z, CHUNKS)),
            dma((n_t,)),
            dma((n_t,)),
            dma((n_t,)),
            dma((n_t,)),
            dma((n_t,)),
            dma((n_t,)),
        ],
        compiler_params=pltpu.CompilerParams(collective_id=0, has_side_effects=True),
    )(live, lam_index, lambdas, sing.reshape(1, features), y_train, u_train, v_basis, x_test)


def solution(mesh):
    placed = (
        P("tm", None),
        P("tm", "vox"),
        P(),
        P(),
        P("vox"),
        P("vox"),
        P("tm", "vox"),
        P(None, "tm"),
    )
    return jax.shard_map(
        functools.partial(body, mesh.shape["tm"], mesh.shape["vox"]),
        mesh=mesh,
        in_specs=placed,
        out_specs=(P("tm", "vox"), P("tm", "vox")),
        check_vma=False,
    )
```

time: 178 us -> 90.6 us (0.51)
  waiting for transfers between devices: 129 us -> 0 us
  Pallas kernels: 0 us -> 86 us
  matrix products: 15.2 us -> 0 us
  between operations: 15.6 us -> 0.64 us
  local copies, waits for them, and re-layouts: 11.1 us -> 3.71 us
  other arithmetic: 6.63 us -> 0 us
    psum x1 -> x0, waiting for transfers between devices: 105 us -> none  [body(): products = lax.psum(partial_value, 'tm')]
    pallas_call x0 -> x1, Pallas kernels: none -> 86 us  [body(): pl.pallas_call(functools.partial(kernel, n_t, n_v, cap), out_shape=(jax.S...]
    reduce_scatter x1 -> x0, waiting for transfers between devices: 23.4 us -> none  [body(): lax.psum_scatter(partial_test, 'tm', scatter_dimension=0, tiled=True)]
    dot_general x4 -> x0, matrix products: 15.2 us -> none  [the longest x1 6.63 us: body(): lax.dot_general(u_train, responses, (((0,), (0,)), ((), ())), preferred_e...]
    convert_element_type x3 -> x0, other arithmetic: 5.68 us -> none  [the longest x1 3.9 us: body(): filtered = blocks.reshape(row_count, used_columns).astype(jnp.bfloat16)]
    gather x3 -> x0, local copies, waits for them, and re-layouts: 3.07 us -> none  [the longest x2 2.51 us: body(): jnp.take(y_train.reshape(time_rows, block_count, BLK), picked, axis=1)]
    scatter x4 -> x0, local copies, waits for them, and re-layouts: 2.73 us -> none  [expand(): placed.at[:, picked, :].set(values.reshape(row_count, capacity, BLK))]
    unnamed x11 -> x2, local copies, waits for them, and re-layouts: 4.43 us -> 3.71 us
  transfers between devices with their start and end apart: 3 -> 0, of which waited for: 2 -> 0; matrix products, arithmetic and copies ran while one was open for 5% -> 0% of each run, Pallas kernels for 0% -> 0%
where the time goes in v1:
time: 90.6 us; the launch traced here: 90.4 us
  Pallas kernels  86 us (95%)
  local copies, waits for them, and re-layouts  3.71 us (4%)
    pallas_call x1, Pallas kernels, body(): pl.pallas_call(functools.partial(kernel, n_t, n_v, cap), out_shape=(jax.S...  86 us
    unnamed x2, local copies, waits for them, and re-layouts  3.71 us

profile of v1, /device:TPU:0, one launch (start us, length us, event | category | flops | bytes accessed | tf_op | source)
XLA Modules:
  0.0 90.4 jit_solution(16120399818817374916)
XLA Ops:
  0.6 86.0 %shard_map.95 = (bf16[1024,384]{1,0:T(8,128)(2,1)}, bf16[256,384]{1,0:T(8,128)(2,1)}) custom-call(s32[3]{0:T(128)} %live_ref.1, s32[3]{0:T(128)} %index_ref.1, f32[20]{0:T(128)} %lambda_ref.1, f32[1,4096]{1,0:T(1,128)} %bitcast.1, bf16[768,384]{1,0:T(8,128)(2,1)} %y_ref.1, bf16[768,4096]{1,0:T(8,128)(2,1)} %u_ref.1, bf16[1024,512]{1,0:T(8,128)(2,1)} %v_ref.1, ...), custom_call_target="tpu_custom_call" | custom-call | tf_op jit(solution)/shard_map/pallas_call | solution.py:388
  86.7 2.1 %copy.12 = bf16[1024,384]{1,0:T(8,128)(2,1)} copy(bf16[1024,384]{1,0:T(8,128)(2,1)} %get-tuple-element.4) | data formatting | bytes 1572864
  88.7 1.6 %copy.13 = bf16[256,384]{1,0:T(8,128)(2,1)} copy(bf16[256,384]{1,0:T(8,128)(2,1)} %get-tuple-element.5) | data formatting | bytes 393216

commit v2 on v1

--- a/solution.py
+++ b/solution.py
@@ -52,6 +52,13 @@
     ag_recv,
     q_send,
     q_recv,
+    far_filt,
+    far_out,
+    far_in,
+    far_filt_send,
+    far_filt_recv,
+    far_send,
+    far_recv,
 ):
     t = lax.axis_index("tm")
     v = lax.axis_index("vox")
@@ -60,13 +67,24 @@
     mate = z * 2 + 1 - core
     rows_v, depth = v_ref.shape
     blocks = live_ref.shape[0]
-    share = part_own.shape[1]
+    share = part_own.shape[2]
+    half = n_z // 2
+    span = n_t * share
+    first_round = jnp.where(z < half, 1, 0)
+    at_low, at_high = z == 0, z == n_z - 1
+    is_end = at_low | at_high
+    is_helper = (z == 1) | (z == n_z - 2)
+
+    def holds(zz, src):
+        return jnp.logical_not(
+            ((zz == 0) & (src >= half)) | ((zz == n_z - 1) & (src < half))
+        )
     test_rows = pred_out.shape[1]
     rc = rows_v // CHUNKS
 
-    def u_copy(owner):
-        cols = pl.ds(pl.multiple_of(owner * share, share), share)
-        return pltpu.make_async_copy(u_ref.at[:, cols], u_buf.at[:, cols], u_sem.at[owner])
+    def u_copy(r, owner):
+        cols = pl.ds(pl.multiple_of(r * span + owner * share, share), share)
+        return pltpu.make_async_copy(u_ref.at[:, cols], u_buf.at[:, cols], u_sem.at[r, owner])
 
     def own_copy(ch):
         rows = pl.ds(ch * rc, rc)
@@ -111,22 +129,22 @@
     def peer(d):
         return lax.rem(t + d, n_t)
 
-    def part_copy(to, owner):
-        return pltpu.make_async_remote_copy(
-            src_ref=part_out.at[to],
-            dst_ref=part_in.at[owner],
-            send_sem=rs_send.at[to],
-            recv_sem=rs_recv.at[owner],
+    def part_copy(r, to, owner):
+        return pltpu.make_async_remote_copy(
+            src_ref=part_out.at[r, to],
+            dst_ref=part_in.at[r, owner],
+            send_sem=rs_send.at[r, to],
+            recv_sem=rs_recv.at[r, owner],
             device_id={"tm": to},
             device_id_type=MESH,
         )
 
-    def filt_copy(to, owner):
-        return pltpu.make_async_remote_copy(
-            src_ref=filt.at[owner],
-            dst_ref=filt.at[owner],
-            send_sem=ag_send.at[to],
-            recv_sem=ag_recv.at[owner],
+    def filt_copy(r, to, owner):
+        return pltpu.make_async_remote_copy(
+            src_ref=filt.at[r, owner],
+            dst_ref=filt.at[r, owner],
+            send_sem=ag_send.at[r, to],
+            recv_sem=ag_recv.at[r, owner],
             device_id={"tm": to},
             device_id_type=MESH,
         )
@@ -141,8 +159,34 @@
             device_id_type=MESH,
         )
 
-    for d in range(n_t):
-        u_copy(peer((d + 1) % n_t)).start()
+    inward = jnp.where(z < half, 1, -1)
+
+    def far_filt_copy(j, step):
+        rows = pl.ds(j * BLK, BLK)
+        return pltpu.make_async_remote_copy(
+            src_ref=filt.at[first_round, :, rows, :],
+            dst_ref=far_filt.at[:, rows, :],
+            send_sem=far_filt_send.at[j],
+            recv_sem=far_filt_recv.at[j],
+            device_id={"vox": v + 2 * step},
+            device_id_type=MESH,
+        )
+
+    def far_copy(j, ch, step):
+        rows = pl.ds(ch * rc, rc)
+        return pltpu.make_async_remote_copy(
+            src_ref=far_out.at[j, rows],
+            dst_ref=far_in.at[j, rows],
+            send_sem=far_send.at[j, ch],
+            recv_sem=far_recv.at[j, ch],
+            device_id={"vox": v + 2 * step},
+            device_id_type=MESH,
+        )
+
+    rounds = (first_round, 1 - first_round)
+    for r in rounds:
+        for d in range(n_t):
+            u_copy(r, peer((d + 1) % n_t)).start()
 
     barrier = pltpu.get_barrier_semaphore()
     for d in range(1, n_t):
@@ -185,23 +229,50 @@
         [sum(pick[j][i] * y_cols[i] for i in range(blocks)).T for j in range(cap)], axis=0
     ).astype(jnp.bfloat16)
 
-    for d in range(1, n_t + 1):
-        to = peer(d % n_t)
-        u_copy(to).wait()
-
-        def tile(i, _, to=to, d=d):
-            off = pl.multiple_of(i * TILE, TILE)
-            cols = pl.ds(pl.multiple_of(to * share + i * TILE, TILE), TILE)
-            value = jnp.dot(y_t, u_buf[:, cols], preferred_element_type=jnp.float32)
-            if d < n_t:
-                part_out[to, :, pl.ds(off, TILE)] = value.astype(jnp.bfloat16)
-            else:
-                part_own[:, pl.ds(off, TILE)] = value
-            return 0
-
-        lax.fori_loop(0, share // TILE, tile, 0)
-        if d < n_t:
-            part_copy(to, t).start()
+    def make_parts(r):
+        for d in range(1, n_t + 1):
+            to = peer(d % n_t)
+            u_copy(r, to).wait()
+
+            def tile(i, _, to=to, d=d):
+                off = pl.multiple_of(i * TILE, TILE)
+                cols = pl.ds(pl.multiple_of(r * span + to * share + i * TILE, TILE), TILE)
+                value = jnp.dot(y_t, u_buf[:, cols], preferred_element_type=jnp.float32)
+                if d < n_t:
+                    part_out[r, to, :, pl.ds(off, TILE)] = value.astype(jnp.bfloat16)
+                else:
+                    part_own[r, :, pl.ds(off, TILE)] = value
+                return 0
+
+            lax.fori_loop(0, share // TILE, tile, 0)
+
+    def send_parts(r):
+        for d in range(1, n_t):
+            part_copy(r, peer(d), t).start()
+
+    def filter_parts(r):
+        for d in range(1, n_t):
+            part_copy(r, peer(d), peer(d)).wait_recv()
+        for i in range(share // TILE):
+            cols = slice(i * TILE, (i + 1) * TILE)
+            place = pl.multiple_of(r * span + t * share + i * TILE, TILE)
+            sing = sing_ref[:, pl.ds(place, TILE)]
+            for j in range(cap):
+                rows = slice(j * BLK, (j + 1) * BLK)
+                total = part_own[r, rows, cols]
+                for d in range(1, n_t):
+                    total = total + part_in[r, peer(d), rows, cols].astype(jnp.float32)
+                factor = sing / (sing * sing + slot_lam[j]) * slot_live[j]
+                filt[r, t, rows, cols] = (total * factor).astype(jnp.bfloat16)
+        for d in range(1, n_t):
+            filt_copy(r, peer(d), t).start()
+
+    def await_filt(r):
+        for d in range(1, n_t):
+            filt_copy(r, peer(d), peer(d)).wait_recv()
+
+    make_parts(rounds[0])
+    send_parts(rounds[0])
 
     for ch in range(CHUNKS):
         pair_copy(z, ch, True).start()
@@ -209,98 +280,116 @@
     x_copy = pltpu.make_async_copy(x_ref, x_buf, x_sem)
     x_copy.start()
 
+    make_parts(rounds[1])
+
     def relay(s, ch):
         low, high = z - 1 - s, z + 1 + s
 
-        @pl.when(low >= 0)
+        @pl.when((low >= 0) & holds(z, low))
         def _():
             line_copy(low, ch, -1).wait_recv()
 
-            @pl.when(z < n_z - 1)
+            @pl.when((z < n_z - 1) & holds(z + 1, low))
             def _():
                 line_copy(low, ch, 1).start()
 
             pair_copy(low, ch).start()
 
-        @pl.when(high < n_z)
+        @pl.when((high < n_z) & holds(z, high))
         def _():
             line_copy(high, ch, 1).wait_recv()
 
-            @pl.when(z > 0)
+            @pl.when((z > 0) & holds(z - 1, high))
             def _():
                 line_copy(high, ch, -1).start()
 
             pair_copy(high, ch).start()
 
-    for ch in range(CHUNKS // 2):
+    early = CHUNKS // 2
+    for ch in range(early):
         relay(0, ch)
-
-    for d in range(1, n_t):
-        part_copy(peer(d), peer(d)).wait_recv()
-    for i in range(share // TILE):
-        cols = slice(i * TILE, (i + 1) * TILE)
-        sing = sing_ref[:, pl.ds(pl.multiple_of(t * share + i * TILE, TILE), TILE)]
+    filter_parts(rounds[0])
+    send_parts(rounds[1])
+    for ch in range(early, CHUNKS):
+        relay(0, ch)
+    await_filt(rounds[0])
+
+    @pl.when(is_end)
+    def _():
         for j in range(cap):
-            rows = slice(j * BLK, (j + 1) * BLK)
-            total = part_own[rows, cols]
-            for d in range(1, n_t):
-                total = total + part_in[peer(d), rows, cols].astype(jnp.float32)
-            factor = sing / (sing * sing + slot_lam[j]) * slot_live[j]
-            filt[t, rows, cols] = (total * factor).astype(jnp.bfloat16)
-    for d in range(1, n_t):
-        filt_copy(peer(d), t).start()
-
-    for ch in range(CHUNKS // 2, CHUNKS):
-        relay(0, ch)
+            far_filt_copy(j, inward).start()
+
+    for ch in range(early):
+        relay(1, ch)
+    filter_parts(rounds[1])
+    for ch in range(early, CHUNKS):
+        relay(1, ch)
 
     def relay_step(s, _):
         for ch in range(CHUNKS):
             relay(s, ch)
         return 0
 
-    lax.fori_loop(1, n_z - 2, relay_step, 0)
-
-    for d in range(1, n_t):
-        filt_copy(peer(d), peer(d)).wait_recv()
-
-    def term(src, ch):
-        pair_arrival(src, ch).wait_recv()
-        rows = pl.ds(ch * rc, rc)
-        value = None
-        for c in range(2):
-            slot = src * 2 + c
-            start = slot * depth
-            owner = start // share
-            offset = pl.multiple_of(start - owner * share, depth)
-            part = lax.dot_general(
-                v_all[slot, rows, :],
-                filt[owner, :, pl.ds(offset, depth)],
-                (((1,), (1,)), ((), ())),
-                preferred_element_type=jnp.float32,
-            )
-            value = part if value is None else value + part
-        return value
+    lax.fori_loop(2, n_z - 2, relay_step, 0)
 
     for ch in range(CHUNKS):
         own_copy(ch).wait()
-        acc[pl.ds(ch * rc, rc), :] = term(z, ch)
-
-    def add_step(s, _):
-        low, high = z - 1 - s, z + 1 + s
-        for ch in range(CHUNKS):
-            rows = pl.ds(ch * rc, rc)
-
-            @pl.when(low >= 0)
-            def _():
-                acc[rows, :] += term(low, ch)
-
-            @pl.when(high < n_z)
-            def _():
-                acc[rows, :] += term(high, ch)
+
+    def await_pair(src, _):
+        @pl.when(holds(z, src))
+        def _():
+            for ch in range(CHUNKS):
+                pair_arrival(src, ch).wait_recv()
 
         return 0
 
-    lax.fori_loop(0, n_z - 2, add_step, 0)
+    lax.fori_loop(0, n_z, await_pair, 0)
+
+    def product(values, slot, rows, factors):
+        return lax.dot_general(
+            values[slot, rows, :], factors, (((1,), (1,)), ((), ())),
+            preferred_element_type=jnp.float32,
+        )
+
+    def place_of(slot):
+        start = lax.rem(slot * depth, span)
+        owner = start // share
+        return owner, pl.ds(pl.multiple_of(start - owner * share, depth), depth)
+
+    @pl.when(is_helper)
+    def _():
+        base = jnp.where(z == 1, half, 0) * 2
+        for j in range(cap):
+            cols = slice(j * BLK, (j + 1) * BLK)
+            far_filt_copy(j, -inward).wait_recv()
+            for ch in range(CHUNKS):
+                rows = pl.ds(ch * rc, rc)
+                value = jnp.zeros((rc, BLK), jnp.float32)
+                for i in range(2 * half):
+                    owner, inner = place_of(base + i)
+                    value += product(v_all, base + i, rows, far_filt[owner, cols, inner])
+                far_out[j, rows, :] = value.astype(jnp.bfloat16)
+                far_copy(j, ch, -inward).start()
+
+    def add_round(r):
+        def step(i, _):
+            slot = r * half * 2 + i
+            owner, inner = place_of(slot)
+            for ch in range(CHUNKS):
+                rows = pl.ds(ch * rc, rc)
+                acc[rows, :] += product(v_all, slot, rows, filt[r, owner, :, inner])
+            return 0
+
+        lax.fori_loop(0, 2 * half, step, 0)
+
+    acc[...] = jnp.zeros_like(acc)
+
+    @pl.when(jnp.logical_not(is_end))
+    def _():
+        add_round(rounds[0])
+
+    await_filt(rounds[1])
+    add_round(rounds[1])
     x_copy.wait()
 
     def expand(values):
@@ -312,13 +401,12 @@
     def finish(ch):
         rows = slice(ch * rc, (ch + 1) * rc)
 
-        @pl.when(z == 0)
+        @pl.when(is_end)
         def _():
-            acc[rows, :] += term(n_z - 1, ch)
-
-        @pl.when(z == n_z - 1)
-        def _():
-            acc[rows, :] += term(0, ch)
+            for j in range(cap):
+                cols = slice(j * BLK, (j + 1) * BLK)
+                far_copy(j, ch, inward).wait_recv()
+                acc[rows, cols] += far_in[j, rows, :].astype(jnp.float32)
 
         weights = acc[rows, :].astype(jnp.bfloat16)
         for i, block in enumerate(expand(weights.astype(jnp.float32))):
@@ -330,10 +418,7 @@
             pred_acc[...] += value
 
     for ch in range(CHUNKS):
-        relay(n_z - 2, ch)
-        if ch > 0:
-            finish(ch - 1)
-    finish(CHUNKS - 1)
+        finish(ch)
 
     for d in range(1, n_t):
         to = peer(d)
@@ -349,19 +434,34 @@
         pred_ref[:, i * BLK : (i + 1) * BLK] = block.astype(jnp.bfloat16)
 
     for d in range(1, n_t):
-        part_copy(peer(d), t).wait_send()
-        filt_copy(peer(d), t).wait_send()
+        for r in rounds:
+            part_copy(r, peer(d), t).wait_send()
+            filt_copy(r, peer(d), t).wait_send()
         pred_copy(peer(d), t).wait_send()
+
+    @pl.when(is_end)
+    def _():
+        for j in range(cap):
+            far_filt_copy(j, inward).wait_send()
+
+    @pl.when(is_helper)
+    def _():
+        for j in range(cap):
+            for ch in range(CHUNKS):
+                far_copy(j, ch, -inward).wait_send()
 
     def drain(src, _):
         for ch in range(CHUNKS):
-            pair_copy(src, ch).wait_send()
-
-            @pl.when((src <= z) & (z < n_z - 1))
+
+            @pl.when(holds(z, src))
+            def _():
+                pair_copy(src, ch).wait_send()
+
+            @pl.when((src <= z) & (z < n_z - 1) & holds(z, src) & holds(z + 1, src))
             def _():
                 line_copy(src, ch, 1).wait_send()
 
-            @pl.when((src >= z) & (z > 0))
+            @pl.when((src >= z) & (z > 0) & holds(z, src) & holds(z - 1, src))
             def _():
                 line_copy(src, ch, -1).wait_send()
 
@@ -378,7 +478,7 @@
     used = cap * BLK
     rows_v, depth = v_basis.shape
     tests = x_test.shape[0]
-    share = features // n_t
+    share = features // n_t // 2
     n_z = n_v // 2
     low, full = jnp.bfloat16, jnp.float32
     smem = pl.BlockSpec(memory_space=pltpu.SMEM)
@@ -397,15 +497,15 @@
             pltpu.VMEM((time_rows, features), low),
             pltpu.VMEM((tests, rows_v), low),
             pltpu.VMEM((n_v, rows_v, depth), low),
-            pltpu.VMEM((n_t, used, share), low),
-            pltpu.VMEM((n_t, used, share), low),
-            pltpu.VMEM((used, share), full),
-            pltpu.VMEM((n_t, used, share), low),
+            pltpu.VMEM((2, n_t, used, share), low),
+            pltpu.VMEM((2, n_t, used, share), low),
+            pltpu.VMEM((2, used, share), full),
+            pltpu.VMEM((2, n_t, used, share), low),
             pltpu.VMEM((rows_v, used), full),
             pltpu.VMEM((tests, used), full),
             pltpu.VMEM((n_t, tests // n_t, used), low),
             pltpu.VMEM((n_t, tests // n_t, used), low),
-            dma((n_t,)),
+            dma((2, n_t)),
             dma,
             dma((CHUNKS,)),
             dma((n_z, CHUNKS)),
@@ -413,12 +513,19 @@
             dma((n_z, CHUNKS)),
             dma((n_z, CHUNKS)),
             dma((n_z, CHUNKS)),
+            dma((2, n_t)),
+            dma((2, n_t)),
+            dma((2, n_t)),
+            dma((2, n_t)),
             dma((n_t,)),
             dma((n_t,)),
-            dma((n_t,)),
-            dma((n_t,)),
-            dma((n_t,)),
-            dma((n_t,)),
+            pltpu.VMEM((n_t, used, share), low),
+            pltpu.VMEM((cap, rows_v, BLK), low),
+            pltpu.VMEM((cap, rows_v, BLK), low),
+            dma((cap,)),
+            dma((cap,)),
+            dma((cap, CHUNKS)),
+            dma((cap, CHUNKS)),
         ],
         compiler_params=pltpu.CompilerParams(collective_id=0, has_side_effects=True),
     )(live, lam_index, lambdas, sing.reshape(1, features), y_train, u_train, v_basis, x_test)

time: 90.6 us -> 82 us (0.905)
  Pallas kernels: 86 us -> 77.5 us
    pallas_call x1, Pallas kernels: 86 us -> 77.5 us  [body(): pl.pallas_call(functools.partial(kernel, n_t, n_v, cap), out_shape=(jax.S...]
where the time goes in v2:
time: 82 us; the launch traced here: 81.8 us
  Pallas kernels  77.5 us (95%)
  local copies, waits for them, and re-layouts  3.71 us (5%)
    pallas_call x1, Pallas kernels, body(): pl.pallas_call(functools.partial(kernel, n_t, n_v, cap), out_shape=(jax.S...  77.5 us
    unnamed x2, local copies, waits for them, and re-layouts  3.71 us

profile of v2, /device:TPU:0, one launch (start us, length us, event | category | flops | bytes accessed | tf_op | source)
XLA Modules:
  0.0 81.8 jit_solution(13184606216295970938)
XLA Ops:
  0.6 77.5 %shard_map.95 = (bf16[1024,384]{1,0:T(8,128)(2,1)}, bf16[256,384]{1,0:T(8,128)(2,1)}) custom-call(s32[3]{0:T(128)} %live_ref.1, s32[3]{0:T(128)} %index_ref.1, f32[20]{0:T(128)} %lambda_ref.1, f32[1,4096]{1,0:T(1,128)} %bitcast.1, bf16[768,384]{1,0:T(8,128)(2,1)} %y_ref.1, bf16[768,4096]{1,0:T(8,128)(2,1)} %u_ref.1, bf16[1024,512]{1,0:T(8,128)(2,1)} %v_ref.1, ...), custom_call_target="tpu_custom_call" | custom-call | tf_op jit(solution)/shard_map/pallas_call | solution.py:488
  78.1 2.1 %copy.12 = bf16[1024,384]{1,0:T(8,128)(2,1)} copy(bf16[1024,384]{1,0:T(8,128)(2,1)} %get-tuple-element.4) | data formatting | bytes 1572864
  80.2 1.6 %copy.13 = bf16[256,384]{1,0:T(8,128)(2,1)} copy(bf16[256,384]{1,0:T(8,128)(2,1)} %get-tuple-element.5) | data formatting | bytes 393216

commit v3 on v2

--- a/solution.py
+++ b/solution.py
@@ -11,6 +11,25 @@
 CHUNKS = 4
 TILE = 256
 MESH = pl.DeviceIdType.MESH
+
+
+def one_hot(live_ref, cap):
+    blocks = live_ref.shape[0]
+    live = [live_ref[i] for i in range(blocks)]
+    before = [sum(live[:i], jnp.int32(0)) for i in range(blocks)]
+    return [
+        [jnp.where(before[i] == j, live[i], 0).astype(jnp.float32) for i in range(blocks)]
+        for j in range(cap)
+    ]
+
+
+def expand(cap, live_ref, w_in, pred_in, w_ref, pred_ref):
+    pick = one_hot(live_ref, cap)
+    for source, target in ((w_in, w_ref), (pred_in, pred_ref)):
+        values = [source[:, j * BLK : (j + 1) * BLK].astype(jnp.float32) for j in range(cap)]
+        for i in range(live_ref.shape[0]):
+            block = sum(pick[j][i] * values[j] for j in range(cap))
+            target[:, i * BLK : (i + 1) * BLK] = block.astype(target.dtype)
 
 
 def kernel(
@@ -59,6 +78,8 @@
     far_filt_recv,
     far_send,
     far_recv,
+    hand_send,
+    hand_recv,
 ):
     t = lax.axis_index("tm")
     v = lax.axis_index("vox")
@@ -149,6 +170,20 @@
             device_id_type=MESH,
         )
 
+    relayed = n_t == 4
+    near = [t + 1 - 2 * lax.rem(t, 2), lax.rem(t + 2, n_t)] if relayed else [peer(d) for d in range(1, n_t)]
+
+    def relay_copy(r, k, to, owner):
+        rows = pl.ds(k * (filt.shape[2] // 2), filt.shape[2] // 2)
+        return pltpu.make_async_remote_copy(
+            src_ref=filt.at[r, owner, rows],
+            dst_ref=filt.at[r, owner, rows],
+            send_sem=hand_send.at[r, k],
+            recv_sem=hand_recv.at[r, k],
+            device_id={"tm": to},
+            device_id_type=MESH,
+        )
+
     def pred_copy(to, owner):
         return pltpu.make_async_remote_copy(
             src_ref=pred_out.at[to],
@@ -214,12 +249,7 @@
         def _():
             line_copy(z, ch, 1, True).start()
 
-    live = [live_ref[i] for i in range(blocks)]
-    before = [sum(live[:i], jnp.int32(0)) for i in range(blocks)]
-    pick = [
-        [jnp.where(before[i] == j, live[i], 0).astype(jnp.float32) for i in range(blocks)]
-        for j in range(cap)
-    ]
+    pick = one_hot(live_ref, cap)
     lam = [lambda_ref[index_ref[i]] for i in range(blocks)]
     slot_lam = [sum(pick[j][i] * lam[i] for i in range(blocks)) for j in range(cap)]
     slot_live = [sum(pick[j][i] for i in range(blocks)) for j in range(cap)]
@@ -229,7 +259,7 @@
         [sum(pick[j][i] * y_cols[i] for i in range(blocks)).T for j in range(cap)], axis=0
     ).astype(jnp.bfloat16)
 
-    def make_parts(r):
+    def make_parts(r, send):
         for d in range(1, n_t + 1):
             to = peer(d % n_t)
             u_copy(r, to).wait()
@@ -245,6 +275,8 @@
                 return 0
 
             lax.fori_loop(0, share // TILE, tile, 0)
+            if send and d < n_t:
+                part_copy(r, to, t).start()
 
     def send_parts(r):
         for d in range(1, n_t):
@@ -264,15 +296,22 @@
                     total = total + part_in[r, peer(d), rows, cols].astype(jnp.float32)
                 factor = sing / (sing * sing + slot_lam[j]) * slot_live[j]
                 filt[r, t, rows, cols] = (total * factor).astype(jnp.bfloat16)
-        for d in range(1, n_t):
-            filt_copy(r, peer(d), t).start()
+        for to in near:
+            filt_copy(r, to, t).start()
+
+    def forward_filt(r):
+        for to in near:
+            filt_copy(r, to, to).wait_recv()
+        if relayed:
+            for k in range(2):
+                relay_copy(r, k, near[k], near[1 - k]).start()
 
     def await_filt(r):
-        for d in range(1, n_t):
-            filt_copy(r, peer(d), peer(d)).wait_recv()
-
-    make_parts(rounds[0])
-    send_parts(rounds[0])
+        if relayed:
+            for k in range(2):
+                relay_copy(r, k, near[k], n_t - 1 - t).wait_recv()
+
+    make_parts(rounds[0], True)
 
     for ch in range(CHUNKS):
         pair_copy(z, ch, True).start()
@@ -280,7 +319,7 @@
     x_copy = pltpu.make_async_copy(x_ref, x_buf, x_sem)
     x_copy.start()
 
-    make_parts(rounds[1])
+    make_parts(rounds[1], False)
 
     def relay(s, ch):
         low, high = z - 1 - s, z + 1 + s
@@ -304,46 +343,6 @@
                 line_copy(high, ch, -1).start()
 
             pair_copy(high, ch).start()
-
-    early = CHUNKS // 2
-    for ch in range(early):
-        relay(0, ch)
-    filter_parts(rounds[0])
-    send_parts(rounds[1])
-    for ch in range(early, CHUNKS):
-        relay(0, ch)
-    await_filt(rounds[0])
-
-    @pl.when(is_end)
-    def _():
-        for j in range(cap):
-            far_filt_copy(j, inward).start()
-
-    for ch in range(early):
-        relay(1, ch)
-    filter_parts(rounds[1])
-    for ch in range(early, CHUNKS):
-        relay(1, ch)
-
-    def relay_step(s, _):
-        for ch in range(CHUNKS):
-            relay(s, ch)
-        return 0
-
-    lax.fori_loop(2, n_z - 2, relay_step, 0)
-
-    for ch in range(CHUNKS):
-        own_copy(ch).wait()
-
-    def await_pair(src, _):
-        @pl.when(holds(z, src))
-        def _():
-            for ch in range(CHUNKS):
-                pair_arrival(src, ch).wait_recv()
-
-        return 0
-
-    lax.fori_loop(0, n_z, await_pair, 0)
 
     def product(values, slot, rows, factors):
         return lax.dot_general(
@@ -356,13 +355,52 @@
         owner = start // share
         return owner, pl.ds(pl.multiple_of(start - owner * share, depth), depth)
 
-    @pl.when(is_helper)
-    def _():
-        base = jnp.where(z == 1, half, 0) * 2
-        for j in range(cap):
-            cols = slice(j * BLK, (j + 1) * BLK)
-            far_filt_copy(j, -inward).wait_recv()
-            for ch in range(CHUNKS):
+    base = jnp.where(z == 1, half, 0) * 2
+
+    def settle(ch):
+        own_copy(ch).wait()
+
+        def step(src, _):
+            @pl.when(holds(z, src))
+            def _():
+                pair_arrival(src, ch).wait_recv()
+
+            return 0
+
+        lax.fori_loop(0, n_z, step, 0)
+
+    def add_round(r, ch):
+        rows = pl.ds(ch * rc, rc)
+
+        def step(i, value):
+            slot = r * half * 2 + i
+            owner, inner = place_of(slot)
+            return value + product(v_all, slot, rows, filt[r, owner, :, inner])
+
+        value = jnp.zeros((rc, acc.shape[1]), jnp.float32)
+        for i in range(2 * half):
+            value = step(i, value)
+        return value
+
+    def far_half(ch):
+        rows = pl.ds(ch * rc, rc)
+
+        @pl.when(jnp.logical_not(is_end))
+        def _():
+            acc[rows, :] = add_round(rounds[0], ch)
+
+        @pl.when(is_end)
+        def _():
+            acc[rows, :] = jnp.zeros((rc, acc.shape[1]), jnp.float32)
+
+    def help_end(j, chunks):
+        cols = slice(j * BLK, (j + 1) * BLK)
+
+        @pl.when(is_helper)
+        def _():
+            if chunks[0] == 0:
+                far_filt_copy(j, -inward).wait_recv()
+            for ch in chunks:
                 rows = pl.ds(ch * rc, rc)
                 value = jnp.zeros((rc, BLK), jnp.float32)
                 for i in range(2 * half):
@@ -371,35 +409,54 @@
                 far_out[j, rows, :] = value.astype(jnp.bfloat16)
                 far_copy(j, ch, -inward).start()
 
-    def add_round(r):
-        def step(i, _):
-            slot = r * half * 2 + i
-            owner, inner = place_of(slot)
-            for ch in range(CHUNKS):
-                rows = pl.ds(ch * rc, rc)
-                acc[rows, :] += product(v_all, slot, rows, filt[r, owner, :, inner])
-            return 0
-
-        lax.fori_loop(0, 2 * half, step, 0)
-
-    acc[...] = jnp.zeros_like(acc)
-
-    @pl.when(jnp.logical_not(is_end))
+    early, last = CHUNKS // 2, CHUNKS - 1
+    for ch in range(early):
+        relay(0, ch)
+    filter_parts(rounds[0])
+    for ch in range(early, last):
+        relay(0, ch)
+    forward_filt(rounds[0])
+    send_parts(rounds[1])
+    relay(0, last)
+    await_filt(rounds[0])
+
+    @pl.when(is_end)
     def _():
-        add_round(rounds[0])
-
+        for j in range(cap):
+            far_filt_copy(j, inward).start()
+
+    def relay_step(s, _):
+        for ch in range(CHUNKS):
+            relay(s, ch)
+        return 0
+
+    lax.fori_loop(1, n_z - 3, relay_step, 0)
+    for ch in range(early):
+        relay(n_z - 3, ch)
+    filter_parts(rounds[1])
+    for ch in range(early, last):
+        relay(n_z - 3, ch)
+    for ch in range(early):
+        settle(ch)
+        far_half(ch)
+    forward_filt(rounds[1])
+    for ch in range(early, last):
+        settle(ch)
+        far_half(ch)
+    help_end(0, list(range(last)))
+    relay(n_z - 3, last)
+    settle(last)
+    help_end(0, [last])
+    far_half(last)
+    help_end(1, list(range(CHUNKS)))
+    for j in range(2, cap):
+        help_end(j, list(range(CHUNKS)))
     await_filt(rounds[1])
-    add_round(rounds[1])
     x_copy.wait()
-
-    def expand(values):
-        return [
-            sum(pick[j][i] * values[:, j * BLK : (j + 1) * BLK] for j in range(cap))
-            for i in range(blocks)
-        ]
 
     def finish(ch):
         rows = slice(ch * rc, (ch + 1) * rc)
+        acc[rows, :] += add_round(rounds[1], ch)
 
         @pl.when(is_end)
         def _():
@@ -409,8 +466,7 @@
                 acc[rows, cols] += far_in[j, rows, :].astype(jnp.float32)
 
         weights = acc[rows, :].astype(jnp.bfloat16)
-        for i, block in enumerate(expand(weights.astype(jnp.float32))):
-            w_ref[rows, i * BLK : (i + 1) * BLK] = block.astype(jnp.bfloat16)
+        w_ref[rows, :] = weights
         value = jnp.dot(x_buf[:, rows], weights, preferred_element_type=jnp.float32)
         if ch == 0:
             pred_acc[...] = value
@@ -430,14 +486,18 @@
     total = pred_acc[pl.ds(pl.multiple_of(t * test_rows, test_rows), test_rows), :]
     for d in range(1, n_t):
         total = total + pred_in[peer(d)].astype(jnp.float32)
-    for i, block in enumerate(expand(total)):
-        pred_ref[:, i * BLK : (i + 1) * BLK] = block.astype(jnp.bfloat16)
+    pred_ref[...] = total.astype(jnp.bfloat16)
 
     for d in range(1, n_t):
         for r in rounds:
             part_copy(r, peer(d), t).wait_send()
-            filt_copy(r, peer(d), t).wait_send()
         pred_copy(peer(d), t).wait_send()
+    for r in rounds:
+        for to in near:
+            filt_copy(r, to, t).wait_send()
+        if relayed:
+            for k in range(2):
+                relay_copy(r, k, near[k], near[1 - k]).wait_send()
 
     @pl.when(is_end)
     def _():
@@ -485,11 +545,11 @@
     vmem = pl.BlockSpec(memory_space=pltpu.VMEM)
     anywhere = pl.BlockSpec(memory_space=pl.ANY)
     dma = pltpu.SemaphoreType.DMA
-    return pl.pallas_call(
+    weights, predicted = pl.pallas_call(
         functools.partial(kernel, n_t, n_v, cap),
         out_shape=(
-            jax.ShapeDtypeStruct((rows_v, columns), low),
-            jax.ShapeDtypeStruct((tests // n_t, columns), low),
+            jax.ShapeDtypeStruct((rows_v, used), low),
+            jax.ShapeDtypeStruct((tests // n_t, used), low),
         ),
         in_specs=[smem, smem, smem, vmem, vmem, anywhere, anywhere, anywhere],
         out_specs=(vmem, vmem),
@@ -526,9 +586,20 @@
             dma((cap,)),
             dma((cap, CHUNKS)),
             dma((cap, CHUNKS)),
+            dma((2, 2)),
+            dma((2, 2)),
         ],
         compiler_params=pltpu.CompilerParams(collective_id=0, has_side_effects=True),
     )(live, lam_index, lambdas, sing.reshape(1, features), y_train, u_train, v_basis, x_test)
+    return pl.pallas_call(
+        functools.partial(expand, cap),
+        out_shape=(
+            jax.ShapeDtypeStruct((rows_v, columns), low),
+            jax.ShapeDtypeStruct((tests // n_t, columns), low),
+        ),
+        in_specs=[smem, vmem, vmem],
+        out_specs=(vmem, vmem),
+    )(live, weights, predicted)
 
 
 def solution(mesh):

time: 82 us -> 77 us (0.939)
  local copies, waits for them, and re-layouts: 3.71 us -> 0 us
  Pallas kernels: 77.5 us -> 76.2 us
    unnamed x2 -> x0, local copies, waits for them, and re-layouts: 3.71 us -> none
    pallas_call x1, Pallas kernels: 77.5 us -> 74 us  [body(): pl.pallas_call(functools.partial(kernel, n_t, n_v, cap), out_shape=(jax.S...]
    pallas_call x0 -> x1, Pallas kernels: none -> 2.25 us  [body(): pl.pallas_call(functools.partial(expand, cap), out_shape=(jax.ShapeDtypeS...]
where the time goes in v3:
time: 77 us; the launch traced here: 76.9 us
  Pallas kernels  76.2 us (99%)
    pallas_call x1, Pallas kernels, body(): pl.pallas_call(functools.partial(kernel, n_t, n_v, cap), out_shape=(jax.S...  74 us
    pallas_call x1, Pallas kernels, body(): pl.pallas_call(functools.partial(expand, cap), out_shape=(jax.ShapeDtypeS...  2.25 us

profile of v3, /device:TPU:0, one launch (start us, length us, event | category | flops | bytes accessed | tf_op | source)
XLA Modules:
  0.0 76.9 jit_solution(14210874723482037052)
XLA Ops:
  0.6 74.0 %shard_map.95 = (bf16[1024,256]{1,0:T(8,128)(2,1)}, bf16[256,256]{1,0:T(8,128)(2,1)}) custom-call(s32[3]{0:T(128)} %live_ref.3, s32[3]{0:T(128)} %index_ref.1, f32[20]{0:T(128)} %lambda_ref.1, f32[1,4096]{1,0:T(1,128)} %bitcast.1, bf16[768,384]{1,0:T(8,128)(2,1)} %y_ref.1, bf16[768,4096]{1,0:T(8,128)(2,1)} %u_ref.1, bf16[1024,512]{1,0:T(8,128)(2,1)} %v_ref.1, ...), custom_call_target="tpu_custom_call" | custom-call | tf_op jit(solution)/shard_map/pallas_call | solution.py:548
  74.6 2.2 %shard_map.96 = (bf16[1024,384]{1,0:T(8,128)(2,1)}, bf16[256,384]{1,0:T(8,128)(2,1)}) custom-call(s32[3]{0:T(128)} %live_ref.3, bf16[1024,256]{1,0:T(8,128)(2,1)} %get-tuple-element.4.w_in, bf16[256,256]{1,0:T(8,128)(2,1)} %get-tuple-element.5.pred_in), custom_call_target="tpu_custom_call" | custom-call | tf_op jit(solution)/shard_map/pallas_call | solution.py:594
